TPU v7x, 32 devices: a whole 2x2x4 slice. The times are simulated.
32 devices in a mesh: ctx: 16 (over z, y, core), wsh: 2 (over x).
Axes of the slice: x: 2, y: 2, z: 4, core: 2. Of those that a mesh axis runs over, the one named last changes fastest.
Arguments:
- tokens: bfloat16 [2, 4096, 1472], P('wsh', 'ctx'), may hold values from -6 to 6
- lengths: int32 [2, 1], P('wsh'), may hold values from 1024 to 4096, as said below
- buckets: int32 [255], replicated, may hold values from 0 to 31, as said below
- attention_gain: bfloat16 [1472], P('wsh'), may hold values from 0.5 to 1.5
- query_weight: bfloat16 [1472, 384], P('wsh'), may hold values from -0.078125 to 0.078125
- key_weight: bfloat16 [1472, 384], P('wsh'), may hold values from -0.078125 to 0.078125
- value_weight: bfloat16 [1472, 384], P('wsh'), may hold values from -0.15625 to 0.15625
- output_weight: bfloat16 [384, 1472], P(None, 'wsh'), may hold values from -2.5 to 2.5
- bias_table: bfloat16 [32, 6], P('wsh'), may hold values from -3 to 3
- feed_gain: bfloat16 [1472], P('wsh'), may hold values from 0.5 to 1.5
- gate_weight: bfloat16 [1472, 3584], P(None, 'wsh'), may hold values from -0.15625 to 0.15625
- up_weight: bfloat16 [1472, 3584], P(None, 'wsh'), may hold values from -0.15625 to 0.15625
- down_weight: bfloat16 [3584, 1472], P('wsh'), may hold values from -0.09375 to 0.09375
- cotangent: bfloat16 [2, 4096, 1472], P('wsh', 'ctx'), may hold values from -6 to 6
Outputs:
- result: bfloat16 [2, 4096, 1472], P('wsh', 'ctx')
- input_gradient: bfloat16 [2, 4096, 1472], P('wsh', 'ctx')
- attention_gain_gradient: float32 [1472], P('wsh')
- query_gradient: float32 [1472, 384], P('wsh', 'ctx')
- key_gradient: float32 [1472, 384], P('wsh', 'ctx')
- value_gradient: float32 [1472, 384], P('wsh', 'ctx')
- output_gradient: float32 [384, 1472], P('ctx', 'wsh')
- bias_gradient: float32 [32, 6], P('wsh')
- feed_gain_gradient: float32 [1472], P('wsh')
- gate_gradient: float32 [1472, 3584], P(None, ('ctx', 'wsh'))
- up_gradient: float32 [1472, 3584], P(None, ('ctx', 'wsh'))
- down_gradient: float32 [3584, 1472], P(('ctx', 'wsh'))
Inputs may be any that keep to these rules, and one draw needn't show every extreme that they name: `lengths`: every sequence has 1024 or more live tokens; in every draw one sequence has all 4096. Offsets j - i <= 0 map into buckets below 16, offsets above 0 into the upper half.
All inputs are finite; a program needn't handle non-finite values.
Results may differ from a plain program's by a relative error of at most 0.02.
Values may be sent and summed in bfloat16 or wider, within the bound.
No kernel may reach another device: no remote copies, remote signals or barrier semaphores. Data moves between devices by JAX's collectives and lax.ppermute only.
A program may use at most 256 MiB of HBM per device.

v0:
```python
import jax
import jax.numpy as jnp
from jax import lax
from jax.sharding import PartitionSpec as P

EPSILON = 1e-06
MASKED = -1e30
HIGH = lax.Precision.HIGHEST


def shifted(block, axis, distance):
    devices = range(lax.axis_size(axis))
    route = [((i - distance) % len(devices), i) for i in devices]
    return lax.ppermute(block, axis, route)


def row_scale(values):
    return lax.rsqrt(jnp.mean(values * values, axis=-1, keepdims=True) + EPSILON)


def normalize(values, gain):
    return values * row_scale(values) * gain


def skew_expand(offset_bias, length):
    count = offset_bias.shape[0]
    padded = jnp.pad(offset_bias, ((0, 0), (0, 1)))
    tiled = jnp.tile(padded, (1, length))[:, : length * (2 * length - 1)]
    return tiled.reshape(count, length, 2 * length - 1)[:, :, length - 1 :]


def diagonal_sums(grid, length):
    count = grid.shape[0]
    wide = jnp.pad(grid, ((0, 0), (0, 0), (length - 1, 0))).reshape(
        count, length * (2 * length - 1)
    )
    wide = jnp.pad(wide, ((0, 0), (0, length)))
    return jnp.sum(wide.reshape(count, length, 2 * length), axis=1)[:, : 2 * length - 1]


def bucket_onehot(offset_start, length, buckets, bucket_count):
    reach = (buckets.shape[0] + 1) // 2
    offsets = offset_start + jnp.arange(2 * length - 1, dtype=jnp.int32) - (length - 1)
    spots = jnp.clip(offsets, 1 - reach, reach - 1) + (reach - 1)
    table_spots = jnp.arange(buckets.shape[0], dtype=jnp.int32)
    chosen = jnp.sum(jnp.where(spots[:, None] == table_spots[None, :], buckets[None, :], 0), axis=1)
    return chosen[:, None] == jnp.arange(bucket_count, dtype=jnp.int32)[None, :]


def block_scores(query3, keys3, table, onehot, key_live, length):
    scores = jnp.einsum("ihd,jhd->hij", query3, keys3, preferred_element_type=jnp.float32)
    offset_bias = jnp.einsum(
        "ob,bh->ho", onehot.astype(jnp.bfloat16), table, preferred_element_type=jnp.float32
    )
    scores = scores + skew_expand(offset_bias, length)
    return jnp.where(key_live[None, None, :], scores, MASKED)


def body(
    tokens,
    lengths,
    buckets,
    attention_gain,
    query_weight,
    key_weight,
    value_weight,
    output_weight,
    bias_table,
    feed_gain,
    gate_weight,
    up_weight,
    down_weight,
    cotangent,
):
    (
        gain_first,
        query_full,
        key_full,
        value_full,
        output_full,
        table_full,
        gain_second,
        gate_full,
        up_full,
        down_full,
    ) = (
        lax.all_gather(attention_gain, "wsh", axis=0, tiled=True),
        lax.all_gather(query_weight, "wsh", axis=0, tiled=True),
        lax.all_gather(key_weight, "wsh", axis=0, tiled=True),
        lax.all_gather(value_weight, "wsh", axis=0, tiled=True),
        lax.all_gather(output_weight, "wsh", axis=1, tiled=True),
        lax.all_gather(bias_table, "wsh", axis=0, tiled=True),
        lax.all_gather(feed_gain, "wsh", axis=0, tiled=True),
        lax.all_gather(gate_weight, "wsh", axis=1, tiled=True),
        lax.all_gather(up_weight, "wsh", axis=1, tiled=True),
        lax.all_gather(down_weight, "wsh", axis=0, tiled=True),
    )
    length = tokens.shape[1]
    heads = table_full.shape[1]
    bucket_count = table_full.shape[0]
    inner = query_full.shape[1]
    head_size = inner // heads
    seq_count = lengths.shape[1]
    wide_count = lax.axis_size("ctx")
    span = wide_count // seq_count
    here = lax.axis_index("ctx")
    my_seq = here % seq_count
    my_block = here // seq_count
    seq_pick = jnp.arange(seq_count, dtype=jnp.int32) == my_seq
    my_length = jnp.sum(jnp.where(seq_pick, lengths[0], 0))
    positions = jnp.arange(length, dtype=jnp.int32)
    live = (my_block * length + positions < my_length).astype(jnp.float32)[:, None]
    inputs = tokens[0].astype(jnp.float32)
    gain_one = gain_first.astype(jnp.float32)
    first = normalize(inputs, gain_one).astype(jnp.bfloat16)
    query = jnp.dot(first, query_full, preferred_element_type=jnp.float32).astype(jnp.bfloat16)
    keys = jnp.dot(first, key_full, preferred_element_type=jnp.float32).astype(jnp.bfloat16)
    values = jnp.dot(first, value_full, preferred_element_type=jnp.float32).astype(jnp.bfloat16)
    query3 = query.reshape(length, heads, head_size)

    def forward_step(carry, block_keys, block_values, key_block):
        run_max, run_total, running = carry
        onehot = bucket_onehot((key_block - my_block) * length, length, buckets, bucket_count)
        key_live = key_block * length + positions < my_length
        scores = block_scores(
            query3,
            block_keys.reshape(length, heads, head_size),
            table_full,
            onehot,
            key_live,
            length,
        )
        new_max = jnp.maximum(run_max, jnp.max(scores, axis=2))
        weights = jnp.exp(scores - new_max[:, :, None])
        factor = jnp.exp(run_max - new_max)
        run_total = run_total * factor + jnp.sum(weights, axis=2)
        update = jnp.einsum(
            "hij,jhd->ihd",
            weights.astype(jnp.bfloat16),
            block_values.reshape(length, heads, head_size),
            preferred_element_type=jnp.float32,
        )
        running = running * jnp.transpose(factor)[:, :, None] + update
        return (new_max, run_total, running)

    start_carry = (
        jnp.full((heads, length), MASKED, jnp.float32),
        jnp.zeros((heads, length), jnp.float32),
        jnp.zeros((length, heads, head_size), jnp.float32),
    )
    start_carry = forward_step(start_carry, keys, values, my_block)
    stored = ()

    def cycle_turn(turn, state):
        carry, block_keys, block_values, stored_blocks = state
        block_keys, block_values = shifted((block_keys, block_values), "ctx", seq_count)
        carry = forward_step(carry, block_keys, block_values, (my_block - turn) % span)
        return (carry, block_keys, block_values, stored_blocks)

    (run_max, run_total, running), _, _, stored = lax.fori_loop(
        1, span, cycle_turn, (start_carry, keys, values, stored)
    )
    log_total = run_max + jnp.log(run_total)
    attention = (running / jnp.transpose(run_total)[:, :, None]).reshape(length, inner)
    attention_low = attention.astype(jnp.bfloat16)
    branch = jnp.dot(attention_low, output_full, preferred_element_type=jnp.float32)
    middle = inputs + live * branch
    gain_two = gain_second.astype(jnp.float32)
    second = normalize(middle, gain_two).astype(jnp.bfloat16)
    gate = jnp.dot(second, gate_full, preferred_element_type=jnp.float32)
    up = jnp.dot(second, up_full, preferred_element_type=jnp.float32)
    hidden = (jax.nn.gelu(gate, approximate=True) * up).astype(jnp.bfloat16)
    feed = jnp.dot(hidden, down_full, preferred_element_type=jnp.float32)
    result = (middle + live * feed).astype(jnp.bfloat16)
    outer = live * cotangent[0].astype(jnp.float32)
    outer_low = outer.astype(jnp.bfloat16)
    down_grad = jnp.einsum("tf,td->fd", hidden, outer_low, preferred_element_type=jnp.float32)
    hidden_grad = jnp.einsum("td,fd->tf", outer_low, down_full, preferred_element_type=jnp.float32)

    def gated(gate_in, up_in):
        return jax.nn.gelu(gate_in, approximate=True) * up_in

    _, gate_pull = jax.vjp(gated, gate, up)
    gate_back, up_back = gate_pull(hidden_grad)
    gate_low = gate_back.astype(jnp.bfloat16)
    up_low = up_back.astype(jnp.bfloat16)
    gate_grad = jnp.einsum("td,tf->df", second, gate_low, preferred_element_type=jnp.float32)
    up_grad = jnp.einsum("td,tf->df", second, up_low, preferred_element_type=jnp.float32)
    second_grad = jnp.einsum(
        "tf,df->td", gate_low, gate_full, preferred_element_type=jnp.float32
    ) + jnp.einsum("tf,df->td", up_low, up_full, preferred_element_type=jnp.float32)
    _, norm_pull = jax.vjp(normalize, middle, gain_two)
    middle_back, gain_two_grad = norm_pull(second_grad)
    middle_grad = outer + middle_back
    branch_low = (live * middle_grad).astype(jnp.bfloat16)
    output_grad = jnp.einsum(
        "ti,td->id", attention_low, branch_low, preferred_element_type=jnp.float32
    )
    attention_grad = jnp.einsum(
        "td,id->ti", branch_low, output_full, preferred_element_type=jnp.float32
    ).astype(jnp.bfloat16)
    attention_grad3 = attention_grad.reshape(length, heads, head_size)
    delta = jnp.transpose(
        jnp.sum(
            (attention_grad.astype(jnp.float32) * attention).reshape(length, heads, head_size),
            axis=2,
        )
    )

    def backward_step(block_keys, block_values, key_block):
        keys3 = block_keys.reshape(length, heads, head_size)
        values3 = block_values.reshape(length, heads, head_size)
        onehot = bucket_onehot((key_block - my_block) * length, length, buckets, bucket_count)
        key_live = key_block * length + positions < my_length
        scores = block_scores(query3, keys3, table_full, onehot, key_live, length)
        probs = jnp.exp(scores - log_total[:, :, None])
        prob_grad = jnp.einsum(
            "ihd,jhd->hij", attention_grad3, values3, preferred_element_type=jnp.float32
        )
        score_grad = (probs * (prob_grad - delta[:, :, None])).astype(jnp.bfloat16)
        part_query = jnp.einsum(
            "hij,jhd->ihd", score_grad, keys3, preferred_element_type=jnp.float32
        )
        part_keys = jnp.einsum(
            "hij,ihd->jhd", score_grad, query3, preferred_element_type=jnp.float32
        )
        part_values = jnp.einsum(
            "hij,ihd->jhd",
            probs.astype(jnp.bfloat16),
            attention_grad3,
            preferred_element_type=jnp.float32,
        )
        part_table = jnp.einsum(
            "ho,ob->bh",
            diagonal_sums(score_grad.astype(jnp.float32), length),
            onehot.astype(jnp.float32),
            precision=HIGH,
        )
        return (
            part_query.reshape(length, inner),
            part_keys.reshape(length, inner),
            part_values.reshape(length, inner),
            part_table,
        )

    def back_turn(turn, state):
        block_keys, block_values, keys_sum, values_sum, query_sum, table_sum = state
        part_query, part_keys, part_values, part_table = backward_step(
            block_keys, block_values, (my_block - turn) % span
        )
        keys_next = keys_sum + part_keys
        values_next = values_sum + part_values
        keys_sum, values_sum = (
            shifted(keys_next.astype(jnp.bfloat16), "ctx", seq_count).astype(keys_next.dtype),
            shifted(values_next.astype(jnp.bfloat16), "ctx", seq_count).astype(values_next.dtype),
        )
        block_keys, block_values = shifted((block_keys, block_values), "ctx", seq_count)
        return (
            block_keys,
            block_values,
            keys_sum,
            values_sum,
            query_sum + part_query,
            table_sum + part_table,
        )

    zeros_rows = jnp.zeros((length, inner), jnp.float32)
    back_state = (
        keys,
        values,
        zeros_rows,
        zeros_rows,
        zeros_rows,
        jnp.zeros((bucket_count, heads), jnp.float32),
    )
    _, _, keys_sum, values_sum, query_sum, table_grad = lax.fori_loop(
        0, span, back_turn, back_state
    )
    query_low = query_sum.astype(jnp.bfloat16)
    keys_low = keys_sum.astype(jnp.bfloat16)
    values_low = values_sum.astype(jnp.bfloat16)
    query_grad = jnp.einsum("td,ti->di", first, query_low, preferred_element_type=jnp.float32)
    key_grad = jnp.einsum("td,ti->di", first, keys_low, preferred_element_type=jnp.float32)
    value_grad = jnp.einsum("td,ti->di", first, values_low, preferred_element_type=jnp.float32)
    first_grad = (
        jnp.einsum("ti,di->td", query_low, query_full, preferred_element_type=jnp.float32)
        + jnp.einsum("ti,di->td", keys_low, key_full, preferred_element_type=jnp.float32)
        + jnp.einsum("ti,di->td", values_low, value_full, preferred_element_type=jnp.float32)
    )
    _, first_pull = jax.vjp(normalize, inputs, gain_one)
    inputs_back, gain_one_grad = first_pull(first_grad)
    input_gradient = (middle_grad + inputs_back).astype(jnp.bfloat16)
    small = lax.psum((gain_one_grad, table_grad, gain_two_grad), "ctx")
    wide = (
        lax.psum_scatter(query_grad, "ctx", scatter_dimension=1, tiled=True),
        lax.psum_scatter(key_grad, "ctx", scatter_dimension=1, tiled=True),
        lax.psum_scatter(value_grad, "ctx", scatter_dimension=1, tiled=True),
        lax.psum_scatter(output_grad, "ctx", scatter_dimension=0, tiled=True),
        lax.psum_scatter(gate_grad, "ctx", scatter_dimension=1, tiled=True),
        lax.psum_scatter(up_grad, "ctx", scatter_dimension=1, tiled=True),
        lax.psum_scatter(down_grad, "ctx", scatter_dimension=0, tiled=True),
    )
    final = (
        lax.psum_scatter(
            small[0].astype(jnp.bfloat16), "wsh", scatter_dimension=0, tiled=True
        ).astype(jnp.float32),
        lax.psum_scatter(
            small[1].astype(jnp.bfloat16), "wsh", scatter_dimension=0, tiled=True
        ).astype(jnp.float32),
        lax.psum_scatter(
            small[2].astype(jnp.bfloat16), "wsh", scatter_dimension=0, tiled=True
        ).astype(jnp.float32),
        lax.psum_scatter(
            wide[0].astype(jnp.bfloat16), "wsh", scatter_dimension=0, tiled=True
        ).astype(jnp.float32),
        lax.psum_scatter(
            wide[1].astype(jnp.bfloat16), "wsh", scatter_dimension=0, tiled=True
        ).astype(jnp.float32),
        lax.psum_scatter(
            wide[2].astype(jnp.bfloat16), "wsh", scatter_dimension=0, tiled=True
        ).astype(jnp.float32),
        lax.psum_scatter(
            wide[3].astype(jnp.bfloat16), "wsh", scatter_dimension=1, tiled=True
        ).astype(jnp.float32),
        lax.psum_scatter(
            wide[4].astype(jnp.bfloat16), "wsh", scatter_dimension=1, tiled=True
        ).astype(jnp.float32),
        lax.psum_scatter(
            wide[5].astype(jnp.bfloat16), "wsh", scatter_dimension=1, tiled=True
        ).astype(jnp.float32),
        lax.psum_scatter(
            wide[6].astype(jnp.bfloat16), "wsh", scatter_dimension=0, tiled=True
        ).astype(jnp.float32),
    )
    gain_one_out, table_out, gain_two_out = (final[0], final[1], final[2])
    query_out, key_out, value_out, output_out = (final[3], final[4], final[5], final[6])
    gate_out, up_out, down_out = (final[7], final[8], final[9])
    return (
        result[None],
        input_gradient[None],
        gain_one_out,
        query_out,
        key_out,
        value_out,
        output_out,
        table_out,
        gain_two_out,
        gate_out,
        up_out,
        down_out,
    )


def solution(mesh):
    placed = (
        P("wsh", "ctx", None),
        P("wsh", None),
        P(),
        P("wsh"),
        P("wsh", None),
        P("wsh", None),
        P("wsh", None),
        P(None, "wsh"),
        P("wsh", None),
        P("wsh"),
        P(None, "wsh"),
        P(None, "wsh"),
        P("wsh", None),
        P("wsh", "ctx", None),
    )
    return jax.shard_map(
        body,
        mesh=mesh,
        in_specs=placed,
        out_specs=(
            P("wsh", "ctx", None),
            P("wsh", "ctx", None),
            P("wsh"),
            P("wsh", "ctx"),
            P("wsh", "ctx"),
            P("wsh", "ctx"),
            P("ctx", "wsh"),
            P("wsh", None),
            P("wsh"),
            P(None, ("ctx", "wsh")),
            P(None, ("ctx", "wsh")),
            P(("ctx", "wsh"), None),
        ),
        check_vma=False,
    )
```

profile of v0, /device:TPU:0, one launch (start us, length us, event | category | flops | bytes accessed | tf_op | source)
XLA Modules:
  0.0 2166.0 jit_solution(2266062317483967884)
XLA Ops:
  12.0 5.2 all-gather
  22.4 4.8 reshape.279
  33.7 5.2 all-reduce.11
  43.6 14.7 all-gather.11.cloned.1.call-done
  65.3 16.8 all-gather.13.cloned.1.call-done
  89.0 317.9 %while.50 = (s32[]{:T(128)}, f32[6,256]{1,0:T(8,128)S(1)}, f32[6,256]{1,0:T(8,128)S(1)}, f32[256,6,64]{0,2,1:T(8,128)}, bf16[256,384]{0,1:T(8,128)(2,1)}, /*inde...) while((s32[]{:T(128)}, f32[6,256]{1,0:T(8,128)S(1)}, ...), condition=%wide.region_8.9_spmd.clone, body=%wide.region_4.8_spmd.clone.sunk | while | flops 104222576 | bytes 41623364 | solution.py:160
  95.8 4.8 reshape.332
  117.2 5.7 reshape.332
  139.4 4.8 reshape.332
  160.4 4.8 reshape.332
  181.5 4.8 reshape.332
  202.5 4.8 reshape.332
  223.6 4.8 reshape.332
  243.6 5.4 reshape.332
  265.4 4.8 reshape.332
  286.4 4.8 reshape.332
  307.5 4.8 reshape.332
  328.5 4.8 reshape.332
  349.6 4.8 reshape.332
  370.6 4.8 reshape.332
  392.2 4.8 reshape.332
  411.8 9.1 fusion.83
  421.0 9.1 fusion.84
  430.0 71.0 %all-gather.21.cloned.1.call-done = bf16[3584,1472]{0,1:T(8,128)(2,1)} async-done(((bf16[1792,1472]{0,1:T(8,128)(2,1)}), bf16[3584,1472]{0,1:T(8,128)(2,1)}) %all-gather.21.cloned.1.call-update) | async-done | bytes 10551312 | tf_op jit(solution)/shard_map/all_gather | solution.py:96
  501.1 12.1 multiply_convert_fusion.1
  513.2 7.0 fusion.85
  520.3 4.1 multiply_reduce_fusion
  528.0 569.6 %while.51 = (s32[]{:T(128)}, bf16[256,384]{0,1:T(8,128)(2,1)}, bf16[256,384]{0,1:T(8,128)(2,1)}, f32[256,384]{0,1:T(8,128)}, f32[256,384]{0,1:T(8,128)}, /*index...) while((s32[]{:T(128)}, bf16[256,384]{0,1:T(8,128)(2,1)}, ...), condition=%wide.region_15.16_spmd.clone, body=%wide.region_12.15_spmd.clone.sunk | while | flops 258763216 | bytes 65157164 | solution.py:276
  538.8 4.8 reshape.334
  550.9 4.0 reshape.335
  574.6 4.8 reshape.334
  610.4 4.8 reshape.334
  646.2 4.8 reshape.334
  681.1 4.8 reshape.334
  716.9 4.8 reshape.334
  752.7 4.8 reshape.334
  788.6 4.8 reshape.334
  823.4 4.8 reshape.334
  859.2 4.8 reshape.334
  895.0 4.8 reshape.334
  930.9 4.8 reshape.334
  965.7 4.8 reshape.334
  1001.5 4.8 reshape.334
  1037.4 4.8 reshape.334
  1073.2 4.8 reshape.334
  1111.8 10.9 fusion.86
  1122.8 10.9 fusion.87
  1134.8 10.8 fusion.49
  1151.8 61.6 %all-reduce.9 = (bf16[1472]{0:T(1024)(128)(2,1)S(1)}, bf16[32,6]{0,1:T(8,128)(2,1)S(1)}, bf16[1472]{0:T(1024)(128)(2,1)S(1)}) all-reduce(f32[1472]{0:T(1024)S(1)} %get-tuple-element.870, f32[32,6]{0,1:T(8,128)S(1)} %copy-done.47, f32[1472]{0:T(1024)S(1)} %copy-done.44), channel_id=1, replica_groups=mesh['ctx'=16,'wsh'=2] {'ctx'}, use_global_device_ids=true, to_apply=%region_18.19 | all-reduce | flops 3136 | bytes 18816 | tf_op jit(solution)/shard_map/psum | solution.py:293
  1216.2 14.2 reduce-scatter.28.cloned.1.call-done
  1232.3 63.7 %reduce-scatter.30.cloned.1.call-done = f32[1472,24]{0,1:T(8,128)} async-done(((f32[1472,384]{0,1:T(8,128)}), f32[1472,24]{0,1:T(8,128)}) %reduce-scatter.30.cloned.1.call-update) | async-done | bytes 141328 | tf_op jit(solution)/shard_map/reduce_scatter | solution.py:297
  1297.9 64.4 %reduce-scatter.32.cloned.1.call-done = f32[24,1472]{1,0:T(8,128)} async-done(((f32[384,1472]{1,0:T(8,128)}), f32[24,1472]{1,0:T(8,128)}) %reduce-scatter.32.cloned.1.call-update) | async-done | bytes 141328 | tf_op jit(solution)/shard_map/reduce_scatter | solution.py:298
  1364.2 219.8 %reduce-scatter.34.cloned.1.call-done = f32[1472,224]{0,1:T(8,128)} async-done(((f32[1472,3584]{0,1:T(8,128)}), f32[1472,224]{0,1:T(8,128)}) %reduce-scatter.34.cloned.1.call-update) | async-done | bytes 1318928 | tf_op jit(solution)/shard_map/reduce_scatter | solution.py:299
  1586.3 219.6 %reduce-scatter.38.cloned.1.call-done = f32[1472,224]{0,1:T(8,128)} async-done(((f32[1472,3584]{0,1:T(8,128)}), f32[1472,224]{0,1:T(8,128)}) %reduce-scatter.38.cloned.1.call-update) | async-done | bytes 1318928 | tf_op jit(solution)/shard_map/reduce_scatter | solution.py:300
  1808.8 218.8 %reduce-scatter.42.cloned.1.call-done = f32[224,1472]{1,0:T(8,128)} async-done(((f32[3584,1472]{1,0:T(8,128)}), f32[224,1472]{1,0:T(8,128)}) %reduce-scatter.42.cloned.1.call-update) | async-done | bytes 1318928 | tf_op jit(solution)/shard_map/reduce_scatter | solution.py:301
  2032.6 5.2 all-reduce.10
  2038.5 8.7 fusion.32
  2048.6 6.1 reduce-scatter.46.cloned.1.call-done
  2056.4 13.4 reduce-scatter.48.cloned.1.call-done
  2071.4 13.4 reduce-scatter.50.cloned.1.call-done
  2086.5 13.5 reduce-scatter.52.cloned.1.call-done
  2101.7 17.4 reduce-scatter.36.cloned.1.call-done
  2121.0 17.3 reduce-scatter.40.cloned.1.call-done
  2140.2 16.8 reduce-scatter.44.cloned.1.call-done
  (1507 shorter events, 823.8 us)
Async XLA Ops:
  7.2 33.8 %all-gather.9.cloned.1.call-start = ((), (), s32[]{:S(2)}) async-start(), calls=%async_computation.15 | async-start | bytes 1695744 | tf_op jit(solution)/shard_map/all_gather | solution.py:88
  7.9 50.4 %all-gather.11.cloned.1.call-start = ((), (), s32[]{:S(2)}) async-start(), calls=%async_computation.16 | async-start | bytes 1695744 | tf_op jit(solution)/shard_map/all_gather | solution.py:89
  8.7 73.5 %all-gather.13.cloned.1.call-start = ((), (), s32[]{:S(2)}) async-start(), calls=%async_computation.17 | async-start | bytes 1695744 | tf_op jit(solution)/shard_map/all_gather | solution.py:90
  9.4 399.5 %all-gather.15.cloned.1.call-start = ((), (), s32[]{:S(2)}) async-start(), calls=%async_computation.18 | async-start | bytes 1695744 | tf_op jit(solution)/shard_map/all_gather | solution.py:91
  10.0 401.8 %all-gather.17.cloned.1.call-start = ((), (), s32[]{:S(2)}) async-start(), calls=%async_computation.19 | async-start | bytes 15826944 | tf_op jit(solution)/shard_map/all_gather | solution.py:94
  10.6 410.4 %all-gather.19.cloned.1.call-start = ((), (), s32[]{:S(2)}) async-start(), calls=%async_computation.20 | async-start | bytes 15826944 | tf_op jit(solution)/shard_map/all_gather | solution.py:95
  11.2 489.9 %all-gather.21.cloned.1.call-start = ((), (), s32[]{:S(2)}) async-start(), calls=%async_computation.21 | async-start | bytes 15826944 | tf_op jit(solution)/shard_map/all_gather | solution.py:96
  11.9 1202.3 %reduce-scatter.26.cloned.1.call-start = ((), (), s32[]{:S(2)}) async-start(), calls=%async_computation.22 | async-start | bytes 2506752 | tf_op jit(solution)/shard_map/reduce_scatter | solution.py:295
  89.0 17.4 collective-permute-start.1
  110.1 18.8 collective-permute-start.1
  132.7 17.3 collective-permute-start.1
  153.8 17.3 collective-permute-start.1
  174.8 17.3 collective-permute-start.1
  195.8 17.3 collective-permute-start.1
  300.8 17.3 collective-permute-start.1
  342.9 17.3 collective-permute-start.1
  363.9 17.7 collective-permute-start.1
  385.5 17.4 collective-permute-start.1
  529.1 34.9 %collective-permute-start.2 = (bf16[256,384]{0,1:T(8,128)(2,1)S(1)}, bf16[256,384]{0,1:T(8,128)(2,1)}, u32[]{:S(2)}, u32[]{:S(2)}) collective-permute-start(bf16[256,384]{0,1:T(8,128)(2,1)S(1)} %copy.139), channel_id=1, source_target_pairs={{30,0},{0,2},{2,4},{4,6},{6,8},{8,10},{10,12},{12,14},{14,16},{16,... | collective-permute-start | bytes 589832 | tf_op jit(solution)/shard_map/while/body/eval_jaxpr/ppermute | solution.py:14
  530.7 33.2 %collective-permute-start.3 = (bf16[256,384]{0,1:T(8,128)(2,1)}, bf16[256,384]{0,1:T(8,128)(2,1)}, u32[]{:S(2)}, u32[]{:S(2)}) collective-permute-start(bf16[256,384]{0,1:T(8,128)(2,1)} %copy.140), channel_id=1, source_target_pairs={{30,0},{0,2},{2,4},{4,6},{6,8},{8,10},{10,12},{12,14},{14,16},{16,... | collective-permute-start | bytes 589832 | tf_op jit(solution)/shard_map/while/body/eval_jaxpr/ppermute | solution.py:14
  564.9 34.9 %collective-permute-start.2 = (bf16[256,384]{0,1:T(8,128)(2,1)S(1)}, bf16[256,384]{0,1:T(8,128)(2,1)}, u32[]{:S(2)}, u32[]{:S(2)}) collective-permute-start(bf16[256,384]{0,1:T(8,128)(2,1)S(1)} %copy.139), channel_id=1, source_target_pairs={{30,0},{0,2},{2,4},{4,6},{6,8},{8,10},{10,12},{12,14},{14,16},{16,... | collective-permute-start | bytes 589832 | tf_op jit(solution)/shard_map/while/body/eval_jaxpr/ppermute | solution.py:14
  566.5 33.2 %collective-permute-start.3 = (bf16[256,384]{0,1:T(8,128)(2,1)}, bf16[256,384]{0,1:T(8,128)(2,1)}, u32[]{:S(2)}, u32[]{:S(2)}) collective-permute-start(bf16[256,384]{0,1:T(8,128)(2,1)} %copy.140), channel_id=1, source_target_pairs={{30,0},{0,2},{2,4},{4,6},{6,8},{8,10},{10,12},{12,14},{14,16},{16,... | collective-permute-start | bytes 589832 | tf_op jit(solution)/shard_map/while/body/eval_jaxpr/ppermute | solution.py:14
  600.7 34.9 %collective-permute-start.2 = (bf16[256,384]{0,1:T(8,128)(2,1)S(1)}, bf16[256,384]{0,1:T(8,128)(2,1)}, u32[]{:S(2)}, u32[]{:S(2)}) collective-permute-start(bf16[256,384]{0,1:T(8,128)(2,1)S(1)} %copy.139), channel_id=1, source_target_pairs={{30,0},{0,2},{2,4},{4,6},{6,8},{8,10},{10,12},{12,14},{14,16},{16,... | collective-permute-start | bytes 589832 | tf_op jit(solution)/shard_map/while/body/eval_jaxpr/ppermute | solution.py:14
  602.4 33.2 %collective-permute-start.3 = (bf16[256,384]{0,1:T(8,128)(2,1)}, bf16[256,384]{0,1:T(8,128)(2,1)}, u32[]{:S(2)}, u32[]{:S(2)}) collective-permute-start(bf16[256,384]{0,1:T(8,128)(2,1)} %copy.140), channel_id=1, source_target_pairs={{30,0},{0,2},{2,4},{4,6},{6,8},{8,10},{10,12},{12,14},{14,16},{16,... | collective-permute-start | bytes 589832 | tf_op jit(solution)/shard_map/while/body/eval_jaxpr/ppermute | solution.py:14
  636.5 33.9 %collective-permute-start.2 = (bf16[256,384]{0,1:T(8,128)(2,1)S(1)}, bf16[256,384]{0,1:T(8,128)(2,1)}, u32[]{:S(2)}, u32[]{:S(2)}) collective-permute-start(bf16[256,384]{0,1:T(8,128)(2,1)S(1)} %copy.139), channel_id=1, source_target_pairs={{30,0},{0,2},{2,4},{4,6},{6,8},{8,10},{10,12},{12,14},{14,16},{16,... | collective-permute-start | bytes 589832 | tf_op jit(solution)/shard_map/while/body/eval_jaxpr/ppermute | solution.py:14
  638.2 32.2 %collective-permute-start.3 = (bf16[256,384]{0,1:T(8,128)(2,1)}, bf16[256,384]{0,1:T(8,128)(2,1)}, u32[]{:S(2)}, u32[]{:S(2)}) collective-permute-start(bf16[256,384]{0,1:T(8,128)(2,1)} %copy.140), channel_id=1, source_target_pairs={{30,0},{0,2},{2,4},{4,6},{6,8},{8,10},{10,12},{12,14},{14,16},{16,... | collective-permute-start | bytes 589832 | tf_op jit(solution)/shard_map/while/body/eval_jaxpr/ppermute | solution.py:14
  671.4 34.9 %collective-permute-start.2 = (bf16[256,384]{0,1:T(8,128)(2,1)S(1)}, bf16[256,384]{0,1:T(8,128)(2,1)}, u32[]{:S(2)}, u32[]{:S(2)}) collective-permute-start(bf16[256,384]{0,1:T(8,128)(2,1)S(1)} %copy.139), channel_id=1, source_target_pairs={{30,0},{0,2},{2,4},{4,6},{6,8},{8,10},{10,12},{12,14},{14,16},{16,... | collective-permute-start | bytes 589832 | tf_op jit(solution)/shard_map/while/body/eval_jaxpr/ppermute | solution.py:14
  673.0 33.2 %collective-permute-start.3 = (bf16[256,384]{0,1:T(8,128)(2,1)}, bf16[256,384]{0,1:T(8,128)(2,1)}, u32[]{:S(2)}, u32[]{:S(2)}) collective-permute-start(bf16[256,384]{0,1:T(8,128)(2,1)} %copy.140), channel_id=1, source_target_pairs={{30,0},{0,2},{2,4},{4,6},{6,8},{8,10},{10,12},{12,14},{14,16},{16,... | collective-permute-start | bytes 589832 | tf_op jit(solution)/shard_map/while/body/eval_jaxpr/ppermute | solution.py:14
  707.2 34.9 %collective-permute-start.2 = (bf16[256,384]{0,1:T(8,128)(2,1)S(1)}, bf16[256,384]{0,1:T(8,128)(2,1)}, u32[]{:S(2)}, u32[]{:S(2)}) collective-permute-start(bf16[256,384]{0,1:T(8,128)(2,1)S(1)} %copy.139), channel_id=1, source_target_pairs={{30,0},{0,2},{2,4},{4,6},{6,8},{8,10},{10,12},{12,14},{14,16},{16,... | collective-permute-start | bytes 589832 | tf_op jit(solution)/shard_map/while/body/eval_jaxpr/ppermute | solution.py:14
  708.9 33.2 %collective-permute-start.3 = (bf16[256,384]{0,1:T(8,128)(2,1)}, bf16[256,384]{0,1:T(8,128)(2,1)}, u32[]{:S(2)}, u32[]{:S(2)}) collective-permute-start(bf16[256,384]{0,1:T(8,128)(2,1)} %copy.140), channel_id=1, source_target_pairs={{30,0},{0,2},{2,4},{4,6},{6,8},{8,10},{10,12},{12,14},{14,16},{16,... | collective-permute-start | bytes 589832 | tf_op jit(solution)/shard_map/while/body/eval_jaxpr/ppermute | solution.py:14
  743.0 34.9 %collective-permute-start.2 = (bf16[256,384]{0,1:T(8,128)(2,1)S(1)}, bf16[256,384]{0,1:T(8,128)(2,1)}, u32[]{:S(2)}, u32[]{:S(2)}) collective-permute-start(bf16[256,384]{0,1:T(8,128)(2,1)S(1)} %copy.139), channel_id=1, source_target_pairs={{30,0},{0,2},{2,4},{4,6},{6,8},{8,10},{10,12},{12,14},{14,16},{16,... | collective-permute-start | bytes 589832 | tf_op jit(solution)/shard_map/while/body/eval_jaxpr/ppermute | solution.py:14
  744.7 33.2 %collective-permute-start.3 = (bf16[256,384]{0,1:T(8,128)(2,1)}, bf16[256,384]{0,1:T(8,128)(2,1)}, u32[]{:S(2)}, u32[]{:S(2)}) collective-permute-start(bf16[256,384]{0,1:T(8,128)(2,1)} %copy.140), channel_id=1, source_target_pairs={{30,0},{0,2},{2,4},{4,6},{6,8},{8,10},{10,12},{12,14},{14,16},{16,... | collective-permute-start | bytes 589832 | tf_op jit(solution)/shard_map/while/body/eval_jaxpr/ppermute | solution.py:14
  778.8 33.9 %collective-permute-start.2 = (bf16[256,384]{0,1:T(8,128)(2,1)S(1)}, bf16[256,384]{0,1:T(8,128)(2,1)}, u32[]{:S(2)}, u32[]{:S(2)}) collective-permute-start(bf16[256,384]{0,1:T(8,128)(2,1)S(1)} %copy.139), channel_id=1, source_target_pairs={{30,0},{0,2},{2,4},{4,6},{6,8},{8,10},{10,12},{12,14},{14,16},{16,... | collective-permute-start | bytes 589832 | tf_op jit(solution)/shard_map/while/body/eval_jaxpr/ppermute | solution.py:14
  780.5 32.2 %collective-permute-start.3 = (bf16[256,384]{0,1:T(8,128)(2,1)}, bf16[256,384]{0,1:T(8,128)(2,1)}, u32[]{:S(2)}, u32[]{:S(2)}) collective-permute-start(bf16[256,384]{0,1:T(8,128)(2,1)} %copy.140), channel_id=1, source_target_pairs={{30,0},{0,2},{2,4},{4,6},{6,8},{8,10},{10,12},{12,14},{14,16},{16,... | collective-permute-start | bytes 589832 | tf_op jit(solution)/shard_map/while/body/eval_jaxpr/ppermute | solution.py:14
  813.7 34.9 %collective-permute-start.2 = (bf16[256,384]{0,1:T(8,128)(2,1)S(1)}, bf16[256,384]{0,1:T(8,128)(2,1)}, u32[]{:S(2)}, u32[]{:S(2)}) collective-permute-start(bf16[256,384]{0,1:T(8,128)(2,1)S(1)} %copy.139), channel_id=1, source_target_pairs={{30,0},{0,2},{2,4},{4,6},{6,8},{8,10},{10,12},{12,14},{14,16},{16,... | collective-permute-start | bytes 589832 | tf_op jit(solution)/shard_map/while/body/eval_jaxpr/ppermute | solution.py:14
  815.4 33.2 %collective-permute-start.3 = (bf16[256,384]{0,1:T(8,128)(2,1)}, bf16[256,384]{0,1:T(8,128)(2,1)}, u32[]{:S(2)}, u32[]{:S(2)}) collective-permute-start(bf16[256,384]{0,1:T(8,128)(2,1)} %copy.140), channel_id=1, source_target_pairs={{30,0},{0,2},{2,4},{4,6},{6,8},{8,10},{10,12},{12,14},{14,16},{16,... | collective-permute-start | bytes 589832 | tf_op jit(solution)/shard_map/while/body/eval_jaxpr/ppermute | solution.py:14
  849.5 34.9 %collective-permute-start.2 = (bf16[256,384]{0,1:T(8,128)(2,1)S(1)}, bf16[256,384]{0,1:T(8,128)(2,1)}, u32[]{:S(2)}, u32[]{:S(2)}) collective-permute-start(bf16[256,384]{0,1:T(8,128)(2,1)S(1)} %copy.139), channel_id=1, source_target_pairs={{30,0},{0,2},{2,4},{4,6},{6,8},{8,10},{10,12},{12,14},{14,16},{16,... | collective-permute-start | bytes 589832 | tf_op jit(solution)/shard_map/while/body/eval_jaxpr/ppermute | solution.py:14
  851.2 33.2 %collective-permute-start.3 = (bf16[256,384]{0,1:T(8,128)(2,1)}, bf16[256,384]{0,1:T(8,128)(2,1)}, u32[]{:S(2)}, u32[]{:S(2)}) collective-permute-start(bf16[256,384]{0,1:T(8,128)(2,1)} %copy.140), channel_id=1, source_target_pairs={{30,0},{0,2},{2,4},{4,6},{6,8},{8,10},{10,12},{12,14},{14,16},{16,... | collective-permute-start | bytes 589832 | tf_op jit(solution)/shard_map/while/body/eval_jaxpr/ppermute | solution.py:14
  885.3 34.9 %collective-permute-start.2 = (bf16[256,384]{0,1:T(8,128)(2,1)S(1)}, bf16[256,384]{0,1:T(8,128)(2,1)}, u32[]{:S(2)}, u32[]{:S(2)}) collective-permute-start(bf16[256,384]{0,1:T(8,128)(2,1)S(1)} %copy.139), channel_id=1, source_target_pairs={{30,0},{0,2},{2,4},{4,6},{6,8},{8,10},{10,12},{12,14},{14,16},{16,... | collective-permute-start | bytes 589832 | tf_op jit(solution)/shard_map/while/body/eval_jaxpr/ppermute | solution.py:14
  887.0 33.2 %collective-permute-start.3 = (bf16[256,384]{0,1:T(8,128)(2,1)}, bf16[256,384]{0,1:T(8,128)(2,1)}, u32[]{:S(2)}, u32[]{:S(2)}) collective-permute-start(bf16[256,384]{0,1:T(8,128)(2,1)} %copy.140), channel_id=1, source_target_pairs={{30,0},{0,2},{2,4},{4,6},{6,8},{8,10},{10,12},{12,14},{14,16},{16,... | collective-permute-start | bytes 589832 | tf_op jit(solution)/shard_map/while/body/eval_jaxpr/ppermute | solution.py:14
  921.2 33.9 %collective-permute-start.2 = (bf16[256,384]{0,1:T(8,128)(2,1)S(1)}, bf16[256,384]{0,1:T(8,128)(2,1)}, u32[]{:S(2)}, u32[]{:S(2)}) collective-permute-start(bf16[256,384]{0,1:T(8,128)(2,1)S(1)} %copy.139), channel_id=1, source_target_pairs={{30,0},{0,2},{2,4},{4,6},{6,8},{8,10},{10,12},{12,14},{14,16},{16,... | collective-permute-start | bytes 589832 | tf_op jit(solution)/shard_map/while/body/eval_jaxpr/ppermute | solution.py:14
  922.8 32.2 %collective-permute-start.3 = (bf16[256,384]{0,1:T(8,128)(2,1)}, bf16[256,384]{0,1:T(8,128)(2,1)}, u32[]{:S(2)}, u32[]{:S(2)}) collective-permute-start(bf16[256,384]{0,1:T(8,128)(2,1)} %copy.140), channel_id=1, source_target_pairs={{30,0},{0,2},{2,4},{4,6},{6,8},{8,10},{10,12},{12,14},{14,16},{16,... | collective-permute-start | bytes 589832 | tf_op jit(solution)/shard_map/while/body/eval_jaxpr/ppermute | solution.py:14
  956.0 34.9 %collective-permute-start.2 = (bf16[256,384]{0,1:T(8,128)(2,1)S(1)}, bf16[256,384]{0,1:T(8,128)(2,1)}, u32[]{:S(2)}, u32[]{:S(2)}) collective-permute-start(bf16[256,384]{0,1:T(8,128)(2,1)S(1)} %copy.139), channel_id=1, source_target_pairs={{30,0},{0,2},{2,4},{4,6},{6,8},{8,10},{10,12},{12,14},{14,16},{16,... | collective-permute-start | bytes 589832 | tf_op jit(solution)/shard_map/while/body/eval_jaxpr/ppermute | solution.py:14
  957.7 33.2 %collective-permute-start.3 = (bf16[256,384]{0,1:T(8,128)(2,1)}, bf16[256,384]{0,1:T(8,128)(2,1)}, u32[]{:S(2)}, u32[]{:S(2)}) collective-permute-start(bf16[256,384]{0,1:T(8,128)(2,1)} %copy.140), channel_id=1, source_target_pairs={{30,0},{0,2},{2,4},{4,6},{6,8},{8,10},{10,12},{12,14},{14,16},{16,... | collective-permute-start | bytes 589832 | tf_op jit(solution)/shard_map/while/body/eval_jaxpr/ppermute | solution.py:14
  991.8 34.9 %collective-permute-start.2 = (bf16[256,384]{0,1:T(8,128)(2,1)S(1)}, bf16[256,384]{0,1:T(8,128)(2,1)}, u32[]{:S(2)}, u32[]{:S(2)}) collective-permute-start(bf16[256,384]{0,1:T(8,128)(2,1)S(1)} %copy.139), channel_id=1, source_target_pairs={{30,0},{0,2},{2,4},{4,6},{6,8},{8,10},{10,12},{12,14},{14,16},{16,... | collective-permute-start | bytes 589832 | tf_op jit(solution)/shard_map/while/body/eval_jaxpr/ppermute | solution.py:14
  993.5 33.2 %collective-permute-start.3 = (bf16[256,384]{0,1:T(8,128)(2,1)}, bf16[256,384]{0,1:T(8,128)(2,1)}, u32[]{:S(2)}, u32[]{:S(2)}) collective-permute-start(bf16[256,384]{0,1:T(8,128)(2,1)} %copy.140), channel_id=1, source_target_pairs={{30,0},{0,2},{2,4},{4,6},{6,8},{8,10},{10,12},{12,14},{14,16},{16,... | collective-permute-start | bytes 589832 | tf_op jit(solution)/shard_map/while/body/eval_jaxpr/ppermute | solution.py:14
  1027.6 34.9 %collective-permute-start.2 = (bf16[256,384]{0,1:T(8,128)(2,1)S(1)}, bf16[256,384]{0,1:T(8,128)(2,1)}, u32[]{:S(2)}, u32[]{:S(2)}) collective-permute-start(bf16[256,384]{0,1:T(8,128)(2,1)S(1)} %copy.139), channel_id=1, source_target_pairs={{30,0},{0,2},{2,4},{4,6},{6,8},{8,10},{10,12},{12,14},{14,16},{16,... | collective-permute-start | bytes 589832 | tf_op jit(solution)/shard_map/while/body/eval_jaxpr/ppermute | solution.py:14
  1029.3 33.2 %collective-permute-start.3 = (bf16[256,384]{0,1:T(8,128)(2,1)}, bf16[256,384]{0,1:T(8,128)(2,1)}, u32[]{:S(2)}, u32[]{:S(2)}) collective-permute-start(bf16[256,384]{0,1:T(8,128)(2,1)} %copy.140), channel_id=1, source_target_pairs={{30,0},{0,2},{2,4},{4,6},{6,8},{8,10},{10,12},{12,14},{14,16},{16,... | collective-permute-start | bytes 589832 | tf_op jit(solution)/shard_map/while/body/eval_jaxpr/ppermute | solution.py:14
  1063.5 33.9 %collective-permute-start.2 = (bf16[256,384]{0,1:T(8,128)(2,1)S(1)}, bf16[256,384]{0,1:T(8,128)(2,1)}, u32[]{:S(2)}, u32[]{:S(2)}) collective-permute-start(bf16[256,384]{0,1:T(8,128)(2,1)S(1)} %copy.139), channel_id=1, source_target_pairs={{30,0},{0,2},{2,4},{4,6},{6,8},{8,10},{10,12},{12,14},{14,16},{16,... | collective-permute-start | bytes 589832 | tf_op jit(solution)/shard_map/while/body/eval_jaxpr/ppermute | solution.py:14
  1065.2 32.2 %collective-permute-start.3 = (bf16[256,384]{0,1:T(8,128)(2,1)}, bf16[256,384]{0,1:T(8,128)(2,1)}, u32[]{:S(2)}, u32[]{:S(2)}) collective-permute-start(bf16[256,384]{0,1:T(8,128)(2,1)} %copy.140), channel_id=1, source_target_pairs={{30,0},{0,2},{2,4},{4,6},{6,8},{8,10},{10,12},{12,14},{14,16},{16,... | collective-permute-start | bytes 589832 | tf_op jit(solution)/shard_map/while/body/eval_jaxpr/ppermute | solution.py:14
  1100.8 129.5 %reduce-scatter.28.cloned.1.call-start = ((), (), s32[]{:S(2)}) async-start(), calls=%async_computation.23 | async-start | bytes 2506752 | tf_op jit(solution)/shard_map/reduce_scatter | solution.py:296
  1104.2 191.7 %reduce-scatter.30.cloned.1.call-start = ((), (), s32[]{:S(2)}) async-start(), calls=%async_computation.24 | async-start | bytes 2506752 | tf_op jit(solution)/shard_map/reduce_scatter | solution.py:297
  1107.3 255.0 %reduce-scatter.32.cloned.1.call-start = ((), (), s32[]{:S(2)}) async-start(), calls=%async_computation.25 | async-start | bytes 2506752 | tf_op jit(solution)/shard_map/reduce_scatter | solution.py:298
  1110.7 473.2 %reduce-scatter.34.cloned.1.call-start = ((), (), s32[]{:S(2)}) async-start(), calls=%async_computation.26 | async-start | bytes 23396352 | tf_op jit(solution)/shard_map/reduce_scatter | solution.py:299
  1122.8 683.1 %reduce-scatter.38.cloned.1.call-start = ((), (), s32[]{:S(2)}) async-start(), calls=%async_computation.28 | async-start | bytes 23396352 | tf_op jit(solution)/shard_map/reduce_scatter | solution.py:300
  1133.7 893.9 %reduce-scatter.42.cloned.1.call-start = ((), (), s32[]{:S(2)}) async-start(), calls=%async_computation.30 | async-start | bytes 23396352 | tf_op jit(solution)/shard_map/reduce_scatter | solution.py:301
  1145.7 901.6 %reduce-scatter.54.cloned.1.call-start = ((), (), s32[]{:S(2)}) async-start(), calls=%async_computation.36 | async-start | bytes 12288
  1214.1 840.6 %reduce-scatter.46.cloned.1.call-start = ((), (), s32[]{:S(2)}) async-start(), calls=%async_computation.32 | async-start | bytes 565248
  1216.1 853.7 %reduce-scatter.48.cloned.1.call-start = ((), (), s32[]{:S(2)}) async-start(), calls=%async_computation.33 | async-start | bytes 565248
  1232.3 852.6 %reduce-scatter.50.cloned.1.call-start = ((), (), s32[]{:S(2)}) async-start(), calls=%async_computation.34 | async-start | bytes 565248
  1297.9 802.2 %reduce-scatter.52.cloned.1.call-start = ((), (), s32[]{:S(2)}) async-start(), calls=%async_computation.35 | async-start | bytes 565248
  1364.1 755.0 %reduce-scatter.36.cloned.1.call-start = ((), (), s32[]{:S(2)}) async-start(), calls=%async_computation.27 | async-start | bytes 1032192 | tf_op jit(solution)/shard_map/reduce_scatter | solution.py:325
  1586.2 552.1 %reduce-scatter.40.cloned.1.call-start = ((), (), s32[]{:S(2)}) async-start(), calls=%async_computation.29 | async-start | bytes 1032192 | tf_op jit(solution)/shard_map/reduce_scatter | solution.py:328
  1808.1 348.9 %reduce-scatter.44.cloned.1.call-start = ((), (), s32[]{:S(2)}) async-start(), calls=%async_computation.31 | async-start | bytes 1032192 | tf_op jit(solution)/shard_map/reduce_scatter | solution.py:331
  (301 other events, 1805.3 us)
Sparse Core Ops, SparseCore 0:
  9.6 24.9 all-gather.8
  36.0 22.2 all-gather.10
  59.9 22.2 all-gather.12
  83.5 22.2 all-gather.14
  107.2 130.3 all-gather.16
  239.0 130.2 all-gather.18
  370.8 130.2 all-gather.20
  1101.0 62.9 reduce-scatter.25
  1168.2 62.0 reduce-scatter.27
  1234.0 61.9 reduce-scatter.29
  1300.2 61.9 reduce-scatter.31
  1366.3 217.6 reduce-scatter.33
  1588.1 217.6 reduce-scatter.37
  1809.9 217.6 reduce-scatter.41
  2030.2 8.8 reduce-scatter.53
  2041.7 12.9 reduce-scatter.45
  2056.8 12.9 reduce-scatter.47
  2071.9 12.9 reduce-scatter.49
  2087.1 12.9 reduce-scatter.51
  2102.7 16.3 reduce-scatter.35
  2121.9 16.3 reduce-scatter.39
  2140.6 16.3 reduce-scatter.43
where the time goes:
time: 2180 us; the launch traced here: 2170 us
  waiting for transfers between devices  1010 us (46%)
  local copies, waits for them, and re-layouts  598 us (27%)
  matrix products  210 us (10%)
  other arithmetic  181 us (8%)
  blocking collectives  77.2 us (4%)
  starting transfers between devices  70.9 us (3%)
    while x578, local copies, waits for them, and re-layouts  255 us
    reduce_scatter x1, waiting for transfers between devices, body(): lax.psum_scatter(gate_grad, 'ctx', scatter_dimension=1, tiled=True)  220 us
    reduce_scatter x1, waiting for transfers between devices, body(): lax.psum_scatter(up_grad, 'ctx', scatter_dimension=1, tiled=True)  220 us
    reduce_scatter x1, waiting for transfers between devices, body(): lax.psum_scatter(down_grad, 'ctx', scatter_dimension=0, tiled=True)  219 us
    reshape x32, local copies, waits for them, and re-layouts, skew_expand(): return tiled.reshape(count, length, 2 * length - 1)[:, :, length - 1:]  154 us
    slice x32, local copies, waits for them, and re-layouts, skew_expand(): tiled = jnp.tile(padded, (1, length))[:, :length * (2 * length - 1)]  75.3 us
    all_gather x1, waiting for transfers between devices, body(): lax.all_gather(down_weight, 'wsh', axis=0, tiled=True)  71 us
    ppermute x94, starting transfers between devices, shifted(): return lax.ppermute(block, axis, route)  70 us
  transfers between devices with their start and end apart: 116, of which 16 were waited for; matrix products, arithmetic and copies ran while one was open for 43% of the time, Pallas kernels for 0%

commit v1 on v0

--- a/solution.py
+++ b/solution.py
@@ -1,3 +1,4 @@
+import functools
 import jax
 import jax.numpy as jnp
 from jax import lax
@@ -6,6 +7,25 @@
 EPSILON = 1e-06
 MASKED = -1e30
 HIGH = lax.Precision.HIGHEST
+
+
+def frame_arrange(frame_in, axis_tag):
+    tile_out = lax.axis_size(axis_tag)
+    y_new, far_arr = (tile_out, lax.axis_index(axis_tag))
+    z2, e_next = (frame_in, 1)
+    while e_next < y_new:
+        crops = []
+        for d in range(y_new):
+            crops.append((d, d ^ e_next))
+        step_out = lax.ppermute(z2, axis_tag, crops)
+        met_up = jnp.concatenate([z2, step_out], 0)
+        high = jnp.concatenate([step_out, z2], 0)
+        z2 = jnp.where(far_arr & e_next == 0, met_up, high)
+        e_next = 2 * e_next
+    return z2
+
+
+replace_points_now = functools.partial(frame_arrange, axis_tag="wsh")
 
 
 def shifted(block, axis, distance):
@@ -93,7 +113,7 @@
         lax.all_gather(feed_gain, "wsh", axis=0, tiled=True),
         lax.all_gather(gate_weight, "wsh", axis=1, tiled=True),
         lax.all_gather(up_weight, "wsh", axis=1, tiled=True),
-        lax.all_gather(down_weight, "wsh", axis=0, tiled=True),
+        replace_points_now(down_weight),
     )
     length = tokens.shape[1]
     heads = table_full.shape[1]

time: 2180 us -> 2240 us (1.028)
  blocking collectives: 77.2 us -> 238 us
  waiting for transfers between devices: 1010 us -> 901 us
    all_gather x1, blocking collectives: 5.23 us -> 167 us  [body(): lax.all_gather(bias_table, 'wsh', axis=0, tiled=True)]
    all_gather x1 -> x0, waiting for transfers between devices: 71 us -> none  [body(): lax.all_gather(down_weight, 'wsh', axis=0, tiled=True)]
    unnamed x27 -> x26, waiting for transfers between devices: 51 us -> 56.1 us
  transfers between devices with their start and end apart: 116 -> 116, of which waited for: 16 -> 13; matrix products, arithmetic and copies ran while one was open for 43% -> 41% of each run, Pallas kernels for 0% -> 0%
where the time goes in v1:
time: 2240 us; the launch traced here: 2230 us
  waiting for transfers between devices  901 us (40%)
  local copies, waits for them, and re-layouts  593 us (26%)
  blocking collectives  238 us (11%)
  matrix products  216 us (10%)
  other arithmetic  181 us (8%)
  starting transfers between devices  74.6 us (3%)
    while x578, local copies, waits for them, and re-layouts  253 us
    reduce_scatter x1, waiting for transfers between devices, body(): lax.psum_scatter(gate_grad, 'ctx', scatter_dimension=1, tiled=True)  220 us
    reduce_scatter x1, waiting for transfers between devices, body(): lax.psum_scatter(up_grad, 'ctx', scatter_dimension=1, tiled=True)  219 us
    reduce_scatter x1, waiting for transfers between devices, body(): lax.psum_scatter(down_grad, 'ctx', scatter_dimension=0, tiled=True)  210 us
    all_gather x1, blocking collectives, body(): lax.all_gather(bias_table, 'wsh', axis=0, tiled=True)  167 us
    reshape x32, local copies, waits for them, and re-layouts, skew_expand(): return tiled.reshape(count, length, 2 * length - 1)[:, :, length - 1:]  153 us
    slice x32, local copies, waits for them, and re-layouts, skew_expand(): tiled = jnp.tile(padded, (1, length))[:, :length * (2 * length - 1)]  72.6 us
    ppermute x94, starting transfers between devices, shifted(): return lax.ppermute(block, axis, route)  70.8 us
  transfers between devices with their start and end apart: 116, of which 13 were waited for; matrix products, arithmetic and copies ran while one was open for 41% of the time, Pallas kernels for 0%

profile of v1, /device:TPU:0, one launch (start us, length us, event | category | flops | bytes accessed | tf_op | source)
XLA Modules:
  0.0 2227.7 jit_solution(6146108082645566348)
XLA Ops:
  13.8 167.4 %all-gather = bf16[2,16,6]{1,2,0:T(8,128)(2,1)S(1)} all-gather(bf16[1,16,6]{1,2,0:T(8,128)(2,1)S(1)} %bitcast.217), channel_id=1, replica_groups=mesh['ctx'=16,'wsh'=2] {'wsh'}, dimensions={0}, use_global_device_ids=true | all-gather | bytes 576 | tf_op jit(solution)/shard_map/all_gather | solution.py:112
  186.2 4.8 reshape.279
  197.5 5.5 all-reduce.11
  221.5 313.7 %while.50 = (s32[]{:T(128)}, f32[6,256]{1,0:T(8,128)S(1)}, f32[6,256]{1,0:T(8,128)S(1)}, f32[256,6,64]{0,2,1:T(8,128)}, bf16[256,384]{0,1:T(8,128)(2,1)}, /*inde...) while((s32[]{:T(128)}, f32[6,256]{1,0:T(8,128)S(1)}, ...), condition=%wide.region_8.9_spmd.clone, body=%wide.region_4.8_spmd.clone.sunk | while | flops 104222576 | bytes 41623364 | solution.py:180
  228.0 4.8 reshape.332
  249.0 4.8 reshape.332
  269.9 4.8 reshape.332
  290.9 4.8 reshape.332
  312.2 5.2 reshape.332
  333.6 4.8 reshape.332
  354.7 4.8 reshape.332
  374.1 4.8 reshape.332
  394.6 4.8 reshape.332
  415.6 4.8 reshape.332
  436.6 4.8 reshape.332
  457.8 4.8 reshape.332
  478.6 4.8 reshape.332
  499.7 4.8 reshape.332
  520.7 4.8 reshape.332
  540.2 9.1 fusion.85
  549.3 8.9 fusion.86
  558.2 17.2 multiply_convert_fusion.1
  575.4 6.4 fusion.87
  583.5 4.1 multiply_reduce_fusion
  591.1 567.8 %while.51 = (s32[]{:T(128)}, bf16[256,384]{0,1:T(8,128)(2,1)}, bf16[256,384]{0,1:T(8,128)(2,1)}, f32[256,384]{0,1:T(8,128)}, f32[256,384]{0,1:T(8,128)}, /*index...) while((s32[]{:T(128)}, bf16[256,384]{0,1:T(8,128)(2,1)}, ...), condition=%wide.region_15.16_spmd.clone, body=%wide.region_12.15_spmd.clone.sunk | while | flops 258763216 | bytes 65157164 | solution.py:296
  600.4 4.8 reshape.334
  612.3 3.9 reshape.335
  635.9 4.8 reshape.334
  648.2 3.9 reshape.335
  672.1 4.8 reshape.334
  707.9 4.8 reshape.334
  742.3 4.8 reshape.334
  777.8 4.8 reshape.334
  813.9 4.8 reshape.334
  826.1 3.9 reshape.335
  849.7 4.8 reshape.334
  884.2 4.8 reshape.334
  919.6 4.8 reshape.334
  931.9 3.9 reshape.335
  955.8 4.8 reshape.334
  991.6 4.8 reshape.334
  1026.0 4.8 reshape.334
  1061.5 4.8 reshape.334
  1097.6 4.8 reshape.334
  1133.4 4.8 reshape.334
  1173.0 11.2 fusion.88
  1184.2 11.0 fusion.89
  1196.3 10.8 fusion.50
  1213.3 60.6 %all-reduce.9 = (bf16[1472]{0:T(1024)(128)(2,1)S(1)}, bf16[32,6]{0,1:T(8,128)(2,1)S(1)}, bf16[1472]{0:T(1024)(128)(2,1)S(1)}) all-reduce(f32[1472]{0:T(1024)S(1)} %get-tuple-element.870, f32[32,6]{0,1:T(8,128)S(1)} %copy-done.48, f32[1472]{0:T(1024)S(1)} %copy-done.45), channel_id=1, replica_groups=mesh['ctx'=16,'wsh'=2] {'ctx'}, use_global_device_ids=true, to_apply=%region_18.19 | all-reduce | flops 3136 | bytes 18816 | tf_op jit(solution)/shard_map/psum | solution.py:313
  1276.6 15.4 reduce-scatter.28.cloned.1.call-done
  1294.0 63.9 %reduce-scatter.30.cloned.1.call-done = f32[1472,24]{0,1:T(8,128)} async-done(((f32[1472,384]{0,1:T(8,128)}), f32[1472,24]{0,1:T(8,128)}) %reduce-scatter.30.cloned.1.call-update) | async-done | bytes 141328 | tf_op jit(solution)/shard_map/reduce_scatter | solution.py:317
  1359.8 64.2 %reduce-scatter.32.cloned.1.call-done = f32[24,1472]{1,0:T(8,128)} async-done(((f32[384,1472]{1,0:T(8,128)}), f32[24,1472]{1,0:T(8,128)}) %reduce-scatter.32.cloned.1.call-update) | async-done | bytes 141328 | tf_op jit(solution)/shard_map/reduce_scatter | solution.py:318
  1426.0 219.9 %reduce-scatter.34.cloned.1.call-done = f32[1472,224]{0,1:T(8,128)} async-done(((f32[1472,3584]{0,1:T(8,128)}), f32[1472,224]{0,1:T(8,128)}) %reduce-scatter.34.cloned.1.call-update) | async-done | bytes 1318928 | tf_op jit(solution)/shard_map/reduce_scatter | solution.py:319
  1648.2 219.4 %reduce-scatter.38.cloned.1.call-done = f32[1472,224]{0,1:T(8,128)} async-done(((f32[1472,3584]{0,1:T(8,128)}), f32[1472,224]{0,1:T(8,128)}) %reduce-scatter.38.cloned.1.call-update) | async-done | bytes 1318928 | tf_op jit(solution)/shard_map/reduce_scatter | solution.py:320
  1870.5 5.0 all-reduce.10
  1879.0 210.5 %reduce-scatter.42.cloned.1.call-done = f32[224,1472]{1,0:T(8,128)} async-done(((f32[3584,1472]{1,0:T(8,128)}), f32[224,1472]{1,0:T(8,128)}) %reduce-scatter.42.cloned.1.call-update) | async-done | bytes 1318928 | tf_op jit(solution)/shard_map/reduce_scatter | solution.py:321
  2091.8 10.9 fusion.32
  2104.1 12.5 reduce-scatter.46.cloned.1.call-done
  2118.3 13.4 reduce-scatter.48.cloned.1.call-done
  2133.3 13.4 reduce-scatter.50.cloned.1.call-done
  2148.4 13.4 reduce-scatter.52.cloned.1.call-done
  2163.5 17.6 reduce-scatter.36.cloned.1.call-done
  2182.9 17.2 reduce-scatter.40.cloned.1.call-done
  2202.0 16.8 reduce-scatter.44.cloned.1.call-done
  (1501 shorter events, 810.4 us)
Async XLA Ops:
  7.2 197.9 %all-gather.8.cloned.1.call-start = ((), (), s32[]{:S(2)}) async-start(), calls=%async_computation.15 | async-start | bytes 1695744 | tf_op jit(solution)/shard_map/all_gather | solution.py:108
  7.9 199.7 %all-gather.10.cloned.1.call-start = ((), (), s32[]{:S(2)}) async-start(), calls=%async_computation.16 | async-start | bytes 1695744 | tf_op jit(solution)/shard_map/all_gather | solution.py:109
  8.7 206.0 %all-gather.12.cloned.1.call-start = ((), (), s32[]{:S(2)}) async-start(), calls=%async_computation.17 | async-start | bytes 1695744 | tf_op jit(solution)/shard_map/all_gather | solution.py:110
  9.4 527.9 %all-gather.14.cloned.1.call-start = ((), (), s32[]{:S(2)}) async-start(), calls=%async_computation.18 | async-start | bytes 1695744 | tf_op jit(solution)/shard_map/all_gather | solution.py:111
  10.0 530.2 %all-gather.16.cloned.1.call-start = ((), (), s32[]{:S(2)}) async-start(), calls=%async_computation.19 | async-start | bytes 15826944 | tf_op jit(solution)/shard_map/all_gather | solution.py:114
  10.6 538.7 %all-gather.18.cloned.1.call-start = ((), (), s32[]{:S(2)}) async-start(), calls=%async_computation.20 | async-start | bytes 15826944 | tf_op jit(solution)/shard_map/all_gather | solution.py:115
  10.6 547.6 %collective-permute-start.6 = (bf16[1792,1472]{0,1:T(8,128)(2,1)}, bf16[1792,1472]{0,1:T(8,128)(2,1)}, u32[]{:S(2)}, u32[]{:S(2)}) collective-permute-start(bf16[1792,1472]{0,1:T(8,128)(2,1)} %param.30), channel_id=1, source_target_pairs={{0,1},{1,0},{2,3},{3,2},{4,5},{5,4},{6,7},{7,6},{8,9},{9,8},{10,11... | collective-permute-start | bytes 15826952 | tf_op jit(solution)/shard_map/ppermute | solution.py:20
  13.7 1261.0 %reduce-scatter.26.cloned.1.call-start = ((), (), s32[]{:S(2)}) async-start(), calls=%async_computation.21 | async-start | bytes 2506752 | tf_op jit(solution)/shard_map/reduce_scatter | solution.py:315
  242.3 17.2 collective-permute-start.1
  263.3 17.2 collective-permute-start.1
  284.2 17.6 collective-permute-start.1
  305.6 17.6 collective-permute-start.1
  326.9 17.3 collective-permute-start.1
  347.9 17.3 collective-permute-start.1
  408.9 17.2 collective-permute-start.1
  450.9 17.5 collective-permute-start.1
  492.9 17.3 collective-permute-start.1
  514.0 17.3 collective-permute-start.1
  592.2 33.0 %collective-permute-start.2 = (bf16[256,384]{0,1:T(8,128)(2,1)S(1)}, bf16[256,384]{0,1:T(8,128)(2,1)}, u32[]{:S(2)}, u32[]{:S(2)}) collective-permute-start(bf16[256,384]{0,1:T(8,128)(2,1)S(1)} %copy.139), channel_id=1, source_target_pairs={{30,0},{0,2},{2,4},{4,6},{6,8},{8,10},{10,12},{12,14},{14,16},{16,... | collective-permute-start | bytes 589832 | tf_op jit(solution)/shard_map/while/body/eval_jaxpr/ppermute | solution.py:34
  593.9 31.3 %collective-permute-start.3 = (bf16[256,384]{0,1:T(8,128)(2,1)}, bf16[256,384]{0,1:T(8,128)(2,1)}, u32[]{:S(2)}, u32[]{:S(2)}) collective-permute-start(bf16[256,384]{0,1:T(8,128)(2,1)} %copy.140), channel_id=1, source_target_pairs={{30,0},{0,2},{2,4},{4,6},{6,8},{8,10},{10,12},{12,14},{14,16},{16,... | collective-permute-start | bytes 589832 | tf_op jit(solution)/shard_map/while/body/eval_jaxpr/ppermute | solution.py:34
  626.2 34.9 %collective-permute-start.2 = (bf16[256,384]{0,1:T(8,128)(2,1)S(1)}, bf16[256,384]{0,1:T(8,128)(2,1)}, u32[]{:S(2)}, u32[]{:S(2)}) collective-permute-start(bf16[256,384]{0,1:T(8,128)(2,1)S(1)} %copy.139), channel_id=1, source_target_pairs={{30,0},{0,2},{2,4},{4,6},{6,8},{8,10},{10,12},{12,14},{14,16},{16,... | collective-permute-start | bytes 589832 | tf_op jit(solution)/shard_map/while/body/eval_jaxpr/ppermute | solution.py:34
  627.9 33.2 %collective-permute-start.3 = (bf16[256,384]{0,1:T(8,128)(2,1)}, bf16[256,384]{0,1:T(8,128)(2,1)}, u32[]{:S(2)}, u32[]{:S(2)}) collective-permute-start(bf16[256,384]{0,1:T(8,128)(2,1)} %copy.140), channel_id=1, source_target_pairs={{30,0},{0,2},{2,4},{4,6},{6,8},{8,10},{10,12},{12,14},{14,16},{16,... | collective-permute-start | bytes 589832 | tf_op jit(solution)/shard_map/while/body/eval_jaxpr/ppermute | solution.py:34
  662.1 35.0 %collective-permute-start.2 = (bf16[256,384]{0,1:T(8,128)(2,1)S(1)}, bf16[256,384]{0,1:T(8,128)(2,1)}, u32[]{:S(2)}, u32[]{:S(2)}) collective-permute-start(bf16[256,384]{0,1:T(8,128)(2,1)S(1)} %copy.139), channel_id=1, source_target_pairs={{30,0},{0,2},{2,4},{4,6},{6,8},{8,10},{10,12},{12,14},{14,16},{16,... | collective-permute-start | bytes 589832 | tf_op jit(solution)/shard_map/while/body/eval_jaxpr/ppermute | solution.py:34
  663.7 33.4 %collective-permute-start.3 = (bf16[256,384]{0,1:T(8,128)(2,1)}, bf16[256,384]{0,1:T(8,128)(2,1)}, u32[]{:S(2)}, u32[]{:S(2)}) collective-permute-start(bf16[256,384]{0,1:T(8,128)(2,1)} %copy.140), channel_id=1, source_target_pairs={{30,0},{0,2},{2,4},{4,6},{6,8},{8,10},{10,12},{12,14},{14,16},{16,... | collective-permute-start | bytes 589832 | tf_op jit(solution)/shard_map/while/body/eval_jaxpr/ppermute | solution.py:34
  698.1 35.1 %collective-permute-start.2 = (bf16[256,384]{0,1:T(8,128)(2,1)S(1)}, bf16[256,384]{0,1:T(8,128)(2,1)}, u32[]{:S(2)}, u32[]{:S(2)}) collective-permute-start(bf16[256,384]{0,1:T(8,128)(2,1)S(1)} %copy.139), channel_id=1, source_target_pairs={{30,0},{0,2},{2,4},{4,6},{6,8},{8,10},{10,12},{12,14},{14,16},{16,... | collective-permute-start | bytes 589832 | tf_op jit(solution)/shard_map/while/body/eval_jaxpr/ppermute | solution.py:34
  699.8 33.4 %collective-permute-start.3 = (bf16[256,384]{0,1:T(8,128)(2,1)}, bf16[256,384]{0,1:T(8,128)(2,1)}, u32[]{:S(2)}, u32[]{:S(2)}) collective-permute-start(bf16[256,384]{0,1:T(8,128)(2,1)} %copy.140), channel_id=1, source_target_pairs={{30,0},{0,2},{2,4},{4,6},{6,8},{8,10},{10,12},{12,14},{14,16},{16,... | collective-permute-start | bytes 589832 | tf_op jit(solution)/shard_map/while/body/eval_jaxpr/ppermute | solution.py:34
  734.1 33.0 %collective-permute-start.2 = (bf16[256,384]{0,1:T(8,128)(2,1)S(1)}, bf16[256,384]{0,1:T(8,128)(2,1)}, u32[]{:S(2)}, u32[]{:S(2)}) collective-permute-start(bf16[256,384]{0,1:T(8,128)(2,1)S(1)} %copy.139), channel_id=1, source_target_pairs={{30,0},{0,2},{2,4},{4,6},{6,8},{8,10},{10,12},{12,14},{14,16},{16,... | collective-permute-start | bytes 589832 | tf_op jit(solution)/shard_map/while/body/eval_jaxpr/ppermute | solution.py:34
  735.8 31.3 %collective-permute-start.3 = (bf16[256,384]{0,1:T(8,128)(2,1)}, bf16[256,384]{0,1:T(8,128)(2,1)}, u32[]{:S(2)}, u32[]{:S(2)}) collective-permute-start(bf16[256,384]{0,1:T(8,128)(2,1)} %copy.140), channel_id=1, source_target_pairs={{30,0},{0,2},{2,4},{4,6},{6,8},{8,10},{10,12},{12,14},{14,16},{16,... | collective-permute-start | bytes 589832 | tf_op jit(solution)/shard_map/while/body/eval_jaxpr/ppermute | solution.py:34
  768.0 34.9 %collective-permute-start.2 = (bf16[256,384]{0,1:T(8,128)(2,1)S(1)}, bf16[256,384]{0,1:T(8,128)(2,1)}, u32[]{:S(2)}, u32[]{:S(2)}) collective-permute-start(bf16[256,384]{0,1:T(8,128)(2,1)S(1)} %copy.139), channel_id=1, source_target_pairs={{30,0},{0,2},{2,4},{4,6},{6,8},{8,10},{10,12},{12,14},{14,16},{16,... | collective-permute-start | bytes 589832 | tf_op jit(solution)/shard_map/while/body/eval_jaxpr/ppermute | solution.py:34
  769.7 33.2 %collective-permute-start.3 = (bf16[256,384]{0,1:T(8,128)(2,1)}, bf16[256,384]{0,1:T(8,128)(2,1)}, u32[]{:S(2)}, u32[]{:S(2)}) collective-permute-start(bf16[256,384]{0,1:T(8,128)(2,1)} %copy.140), channel_id=1, source_target_pairs={{30,0},{0,2},{2,4},{4,6},{6,8},{8,10},{10,12},{12,14},{14,16},{16,... | collective-permute-start | bytes 589832 | tf_op jit(solution)/shard_map/while/body/eval_jaxpr/ppermute | solution.py:34
  803.9 35.0 %collective-permute-start.2 = (bf16[256,384]{0,1:T(8,128)(2,1)S(1)}, bf16[256,384]{0,1:T(8,128)(2,1)}, u32[]{:S(2)}, u32[]{:S(2)}) collective-permute-start(bf16[256,384]{0,1:T(8,128)(2,1)S(1)} %copy.139), channel_id=1, source_target_pairs={{30,0},{0,2},{2,4},{4,6},{6,8},{8,10},{10,12},{12,14},{14,16},{16,... | collective-permute-start | bytes 589832 | tf_op jit(solution)/shard_map/while/body/eval_jaxpr/ppermute | solution.py:34
  805.6 33.4 %collective-permute-start.3 = (bf16[256,384]{0,1:T(8,128)(2,1)}, bf16[256,384]{0,1:T(8,128)(2,1)}, u32[]{:S(2)}, u32[]{:S(2)}) collective-permute-start(bf16[256,384]{0,1:T(8,128)(2,1)} %copy.140), channel_id=1, source_target_pairs={{30,0},{0,2},{2,4},{4,6},{6,8},{8,10},{10,12},{12,14},{14,16},{16,... | collective-permute-start | bytes 589832 | tf_op jit(solution)/shard_map/while/body/eval_jaxpr/ppermute | solution.py:34
  839.9 35.1 %collective-permute-start.2 = (bf16[256,384]{0,1:T(8,128)(2,1)S(1)}, bf16[256,384]{0,1:T(8,128)(2,1)}, u32[]{:S(2)}, u32[]{:S(2)}) collective-permute-start(bf16[256,384]{0,1:T(8,128)(2,1)S(1)} %copy.139), channel_id=1, source_target_pairs={{30,0},{0,2},{2,4},{4,6},{6,8},{8,10},{10,12},{12,14},{14,16},{16,... | collective-permute-start | bytes 589832 | tf_op jit(solution)/shard_map/while/body/eval_jaxpr/ppermute | solution.py:34
  841.6 33.4 %collective-permute-start.3 = (bf16[256,384]{0,1:T(8,128)(2,1)}, bf16[256,384]{0,1:T(8,128)(2,1)}, u32[]{:S(2)}, u32[]{:S(2)}) collective-permute-start(bf16[256,384]{0,1:T(8,128)(2,1)} %copy.140), channel_id=1, source_target_pairs={{30,0},{0,2},{2,4},{4,6},{6,8},{8,10},{10,12},{12,14},{14,16},{16,... | collective-permute-start | bytes 589832 | tf_op jit(solution)/shard_map/while/body/eval_jaxpr/ppermute | solution.py:34
  875.9 33.0 %collective-permute-start.2 = (bf16[256,384]{0,1:T(8,128)(2,1)S(1)}, bf16[256,384]{0,1:T(8,128)(2,1)}, u32[]{:S(2)}, u32[]{:S(2)}) collective-permute-start(bf16[256,384]{0,1:T(8,128)(2,1)S(1)} %copy.139), channel_id=1, source_target_pairs={{30,0},{0,2},{2,4},{4,6},{6,8},{8,10},{10,12},{12,14},{14,16},{16,... | collective-permute-start | bytes 589832 | tf_op jit(solution)/shard_map/while/body/eval_jaxpr/ppermute | solution.py:34
  877.6 31.3 %collective-permute-start.3 = (bf16[256,384]{0,1:T(8,128)(2,1)}, bf16[256,384]{0,1:T(8,128)(2,1)}, u32[]{:S(2)}, u32[]{:S(2)}) collective-permute-start(bf16[256,384]{0,1:T(8,128)(2,1)} %copy.140), channel_id=1, source_target_pairs={{30,0},{0,2},{2,4},{4,6},{6,8},{8,10},{10,12},{12,14},{14,16},{16,... | collective-permute-start | bytes 589832 | tf_op jit(solution)/shard_map/while/body/eval_jaxpr/ppermute | solution.py:34
  909.9 34.9 %collective-permute-start.2 = (bf16[256,384]{0,1:T(8,128)(2,1)S(1)}, bf16[256,384]{0,1:T(8,128)(2,1)}, u32[]{:S(2)}, u32[]{:S(2)}) collective-permute-start(bf16[256,384]{0,1:T(8,128)(2,1)S(1)} %copy.139), channel_id=1, source_target_pairs={{30,0},{0,2},{2,4},{4,6},{6,8},{8,10},{10,12},{12,14},{14,16},{16,... | collective-permute-start | bytes 589832 | tf_op jit(solution)/shard_map/while/body/eval_jaxpr/ppermute | solution.py:34
  911.6 33.2 %collective-permute-start.3 = (bf16[256,384]{0,1:T(8,128)(2,1)}, bf16[256,384]{0,1:T(8,128)(2,1)}, u32[]{:S(2)}, u32[]{:S(2)}) collective-permute-start(bf16[256,384]{0,1:T(8,128)(2,1)} %copy.140), channel_id=1, source_target_pairs={{30,0},{0,2},{2,4},{4,6},{6,8},{8,10},{10,12},{12,14},{14,16},{16,... | collective-permute-start | bytes 589832 | tf_op jit(solution)/shard_map/while/body/eval_jaxpr/ppermute | solution.py:34
  945.8 35.0 %collective-permute-start.2 = (bf16[256,384]{0,1:T(8,128)(2,1)S(1)}, bf16[256,384]{0,1:T(8,128)(2,1)}, u32[]{:S(2)}, u32[]{:S(2)}) collective-permute-start(bf16[256,384]{0,1:T(8,128)(2,1)S(1)} %copy.139), channel_id=1, source_target_pairs={{30,0},{0,2},{2,4},{4,6},{6,8},{8,10},{10,12},{12,14},{14,16},{16,... | collective-permute-start | bytes 589832 | tf_op jit(solution)/shard_map/while/body/eval_jaxpr/ppermute | solution.py:34
  947.5 33.4 %collective-permute-start.3 = (bf16[256,384]{0,1:T(8,128)(2,1)}, bf16[256,384]{0,1:T(8,128)(2,1)}, u32[]{:S(2)}, u32[]{:S(2)}) collective-permute-start(bf16[256,384]{0,1:T(8,128)(2,1)} %copy.140), channel_id=1, source_target_pairs={{30,0},{0,2},{2,4},{4,6},{6,8},{8,10},{10,12},{12,14},{14,16},{16,... | collective-permute-start | bytes 589832 | tf_op jit(solution)/shard_map/while/body/eval_jaxpr/ppermute | solution.py:34
  981.8 35.1 %collective-permute-start.2 = (bf16[256,384]{0,1:T(8,128)(2,1)S(1)}, bf16[256,384]{0,1:T(8,128)(2,1)}, u32[]{:S(2)}, u32[]{:S(2)}) collective-permute-start(bf16[256,384]{0,1:T(8,128)(2,1)S(1)} %copy.139), channel_id=1, source_target_pairs={{30,0},{0,2},{2,4},{4,6},{6,8},{8,10},{10,12},{12,14},{14,16},{16,... | collective-permute-start | bytes 589832 | tf_op jit(solution)/shard_map/while/body/eval_jaxpr/ppermute | solution.py:34
  983.5 33.4 %collective-permute-start.3 = (bf16[256,384]{0,1:T(8,128)(2,1)}, bf16[256,384]{0,1:T(8,128)(2,1)}, u32[]{:S(2)}, u32[]{:S(2)}) collective-permute-start(bf16[256,384]{0,1:T(8,128)(2,1)} %copy.140), channel_id=1, source_target_pairs={{30,0},{0,2},{2,4},{4,6},{6,8},{8,10},{10,12},{12,14},{14,16},{16,... | collective-permute-start | bytes 589832 | tf_op jit(solution)/shard_map/while/body/eval_jaxpr/ppermute | solution.py:34
  1017.8 33.0 %collective-permute-start.2 = (bf16[256,384]{0,1:T(8,128)(2,1)S(1)}, bf16[256,384]{0,1:T(8,128)(2,1)}, u32[]{:S(2)}, u32[]{:S(2)}) collective-permute-start(bf16[256,384]{0,1:T(8,128)(2,1)S(1)} %copy.139), channel_id=1, source_target_pairs={{30,0},{0,2},{2,4},{4,6},{6,8},{8,10},{10,12},{12,14},{14,16},{16,... | collective-permute-start | bytes 589832 | tf_op jit(solution)/shard_map/while/body/eval_jaxpr/ppermute | solution.py:34
  1019.5 31.3 %collective-permute-start.3 = (bf16[256,384]{0,1:T(8,128)(2,1)}, bf16[256,384]{0,1:T(8,128)(2,1)}, u32[]{:S(2)}, u32[]{:S(2)}) collective-permute-start(bf16[256,384]{0,1:T(8,128)(2,1)} %copy.140), channel_id=1, source_target_pairs={{30,0},{0,2},{2,4},{4,6},{6,8},{8,10},{10,12},{12,14},{14,16},{16,... | collective-permute-start | bytes 589832 | tf_op jit(solution)/shard_map/while/body/eval_jaxpr/ppermute | solution.py:34
  1051.7 34.9 %collective-permute-start.2 = (bf16[256,384]{0,1:T(8,128)(2,1)S(1)}, bf16[256,384]{0,1:T(8,128)(2,1)}, u32[]{:S(2)}, u32[]{:S(2)}) collective-permute-start(bf16[256,384]{0,1:T(8,128)(2,1)S(1)} %copy.139), channel_id=1, source_target_pairs={{30,0},{0,2},{2,4},{4,6},{6,8},{8,10},{10,12},{12,14},{14,16},{16,... | collective-permute-start | bytes 589832 | tf_op jit(solution)/shard_map/while/body/eval_jaxpr/ppermute | solution.py:34
  1053.4 33.2 %collective-permute-start.3 = (bf16[256,384]{0,1:T(8,128)(2,1)}, bf16[256,384]{0,1:T(8,128)(2,1)}, u32[]{:S(2)}, u32[]{:S(2)}) collective-permute-start(bf16[256,384]{0,1:T(8,128)(2,1)} %copy.140), channel_id=1, source_target_pairs={{30,0},{0,2},{2,4},{4,6},{6,8},{8,10},{10,12},{12,14},{14,16},{16,... | collective-permute-start | bytes 589832 | tf_op jit(solution)/shard_map/while/body/eval_jaxpr/ppermute | solution.py:34
  1087.6 35.0 %collective-permute-start.2 = (bf16[256,384]{0,1:T(8,128)(2,1)S(1)}, bf16[256,384]{0,1:T(8,128)(2,1)}, u32[]{:S(2)}, u32[]{:S(2)}) collective-permute-start(bf16[256,384]{0,1:T(8,128)(2,1)S(1)} %copy.139), channel_id=1, source_target_pairs={{30,0},{0,2},{2,4},{4,6},{6,8},{8,10},{10,12},{12,14},{14,16},{16,... | collective-permute-start | bytes 589832 | tf_op jit(solution)/shard_map/while/body/eval_jaxpr/ppermute | solution.py:34
  1089.3 33.4 %collective-permute-start.3 = (bf16[256,384]{0,1:T(8,128)(2,1)}, bf16[256,384]{0,1:T(8,128)(2,1)}, u32[]{:S(2)}, u32[]{:S(2)}) collective-permute-start(bf16[256,384]{0,1:T(8,128)(2,1)} %copy.140), channel_id=1, source_target_pairs={{30,0},{0,2},{2,4},{4,6},{6,8},{8,10},{10,12},{12,14},{14,16},{16,... | collective-permute-start | bytes 589832 | tf_op jit(solution)/shard_map/while/body/eval_jaxpr/ppermute | solution.py:34
  1123.6 35.1 %collective-permute-start.2 = (bf16[256,384]{0,1:T(8,128)(2,1)S(1)}, bf16[256,384]{0,1:T(8,128)(2,1)}, u32[]{:S(2)}, u32[]{:S(2)}) collective-permute-start(bf16[256,384]{0,1:T(8,128)(2,1)S(1)} %copy.139), channel_id=1, source_target_pairs={{30,0},{0,2},{2,4},{4,6},{6,8},{8,10},{10,12},{12,14},{14,16},{16,... | collective-permute-start | bytes 589832 | tf_op jit(solution)/shard_map/while/body/eval_jaxpr/ppermute | solution.py:34
  1125.3 33.4 %collective-permute-start.3 = (bf16[256,384]{0,1:T(8,128)(2,1)}, bf16[256,384]{0,1:T(8,128)(2,1)}, u32[]{:S(2)}, u32[]{:S(2)}) collective-permute-start(bf16[256,384]{0,1:T(8,128)(2,1)} %copy.140), channel_id=1, source_target_pairs={{30,0},{0,2},{2,4},{4,6},{6,8},{8,10},{10,12},{12,14},{14,16},{16,... | collective-permute-start | bytes 589832 | tf_op jit(solution)/shard_map/while/body/eval_jaxpr/ppermute | solution.py:34
  1162.2 129.8 %reduce-scatter.28.cloned.1.call-start = ((), (), s32[]{:S(2)}) async-start(), calls=%async_computation.22 | async-start | bytes 2506752 | tf_op jit(solution)/shard_map/reduce_scatter | solution.py:316
  1165.5 192.4 %reduce-scatter.30.cloned.1.call-start = ((), (), s32[]{:S(2)}) async-start(), calls=%async_computation.23 | async-start | bytes 2506752 | tf_op jit(solution)/shard_map/reduce_scatter | solution.py:317
  1168.5 255.5 %reduce-scatter.32.cloned.1.call-start = ((), (), s32[]{:S(2)}) async-start(), calls=%async_computation.24 | async-start | bytes 2506752 | tf_op jit(solution)/shard_map/reduce_scatter | solution.py:318
  1171.8 474.0 %reduce-scatter.34.cloned.1.call-start = ((), (), s32[]{:S(2)}) async-start(), calls=%async_computation.25 | async-start | bytes 23396352 | tf_op jit(solution)/shard_map/reduce_scatter | solution.py:319
  1184.1 683.4 %reduce-scatter.38.cloned.1.call-start = ((), (), s32[]{:S(2)}) async-start(), calls=%async_computation.27 | async-start | bytes 23396352 | tf_op jit(solution)/shard_map/reduce_scatter | solution.py:320
  1195.2 894.3 %reduce-scatter.42.cloned.1.call-start = ((), (), s32[]{:S(2)}) async-start(), calls=%async_computation.29 | async-start | bytes 23396352 | tf_op jit(solution)/shard_map/reduce_scatter | solution.py:321
  1207.2 895.5 %reduce-scatter.54.cloned.1.call-start = ((), (), s32[]{:S(2)}) async-start(), calls=%async_computation.35 | async-start | bytes 12288
  1274.6 842.0 %reduce-scatter.46.cloned.1.call-start = ((), (), s32[]{:S(2)}) async-start(), calls=%async_computation.31 | async-start | bytes 565248
  1276.6 855.1 %reduce-scatter.48.cloned.1.call-start = ((), (), s32[]{:S(2)}) async-start(), calls=%async_computation.32 | async-start | bytes 565248
  1293.9 852.8 %reduce-scatter.50.cloned.1.call-start = ((), (), s32[]{:S(2)}) async-start(), calls=%async_computation.33 | async-start | bytes 565248
  1359.8 802.0 %reduce-scatter.52.cloned.1.call-start = ((), (), s32[]{:S(2)}) async-start(), calls=%async_computation.34 | async-start | bytes 565248
  1425.9 755.1 %reduce-scatter.36.cloned.1.call-start = ((), (), s32[]{:S(2)}) async-start(), calls=%async_computation.26 | async-start | bytes 1032192 | tf_op jit(solution)/shard_map/reduce_scatter | solution.py:345
  1648.1 552.0 %reduce-scatter.40.cloned.1.call-start = ((), (), s32[]{:S(2)}) async-start(), calls=%async_computation.28 | async-start | bytes 1032192 | tf_op jit(solution)/shard_map/reduce_scatter | solution.py:348
  1869.9 348.9 %reduce-scatter.44.cloned.1.call-start = ((), (), s32[]{:S(2)}) async-start(), calls=%async_computation.30 | async-start | bytes 1032192 | tf_op jit(solution)/shard_map/reduce_scatter | solution.py:351
  (299 other events, 1944.4 us)
Sparse Core Ops, SparseCore 0:
  9.6 37.1 all-gather.7
  48.3 34.4 all-gather.9
  84.3 34.4 all-gather.11
  120.2 34.4 all-gather.13
  156.1 133.3 all-gather.15
  291.0 131.7 all-gather.17
  1162.3 63.3 reduce-scatter.25
  1229.9 62.0 reduce-scatter.27
  1295.8 62.0 reduce-scatter.29
  1362.0 61.9 reduce-scatter.31
  1428.2 217.5 reduce-scatter.33
  1649.9 217.6 reduce-scatter.37
  1871.8 217.6 reduce-scatter.41
  2092.1 8.8 reduce-scatter.53
  2103.6 12.9 reduce-scatter.45
  2118.7 12.9 reduce-scatter.47
  2133.8 12.9 reduce-scatter.49
  2148.8 12.9 reduce-scatter.51
  2164.6 16.3 reduce-scatter.35
  2183.7 16.3 reduce-scatter.39
  2202.4 16.3 reduce-scatter.43
